TPU v7x, 32 devices: a whole 2x2x4 slice. The times are simulated.
32 devices in a mesh: col: 4 (over y, x), row: 8 (over z, core).
Axes of the slice: x: 2, y: 2, z: 4, core: 2. Of those that a mesh axis runs over, the one named last changes fastest.
Arguments:
- covariance: float32 [12288, 12288], P('row', 'col'), may hold values from -2 to 2, as said below
- wfs_map: int32 [12288], P('row'), may hold values from 0 to 5
- noise_var: float32 [6], replicated, may hold values from 0.5 to 2
- targets: float32 [12288, 2048], P('row', 'col'), may hold values from -0.6 to 0.6
- target_pos: float32 [2, 2048], replicated, may hold values from -1 to 1
- layer_strength: float32 [35], replicated, may hold values from 0.005 to 0.05
- layer_scale: float32 [35], replicated, may hold values from 0.2 to 2
- tile_layer: int32 [16], replicated, may hold values from 0 to 34
Outputs:
- updated: float32 [12288, 12288], P('row', 'col')
- panel_factor: float32 [12288, 256], P('row')
- reconstructor: float32 [12288, 2048], P('row', 'col')
- error_cov: float32 [2048, 2048], P('row', 'col')
Inputs may be any that keep to these rules, and one draw needn't show every extreme that they name: `covariance`: symmetric and positive semidefinite; its diagonal lies between 0.5 and 2.
All inputs are finite; a program needn't handle non-finite values.
Results may differ from a plain program's by a relative error of at most 0.0003.
Values sent between devices are 32-bit elements; how exact they have to be, the bound alone decides.
A program may use at most 128 MiB of HBM per device.

v0:
```python
import functools

import jax
import jax.numpy as jnp
from jax import lax
from jax.experimental import pallas as pl
from jax.experimental.pallas import tpu as pltpu
from jax.sharding import PartitionSpec as P

PB = 256
TILE = 128
HALF = PB // 2
CHUNKS = 8
ROW_CHUNKS = 6
SEGMENT = 16

MESH = pl.DeviceIdType.MESH
precise = lax.Precision.HIGHEST


def dot(a, b, dims=((1,), (0,))):
    return lax.dot_general(
        a, b, (dims, ((), ())), precision=precise, preferred_element_type=jnp.float32
    )


def outer(a, b):
    def thirds(x):
        high = x.astype(jnp.bfloat16).astype(jnp.float32)
        middle = (x - high).astype(jnp.bfloat16).astype(jnp.float32)
        return high, middle, x - high - middle

    p, q = thirds(a), thirds(b)
    left = jnp.concatenate([p[0], p[0], p[1], p[0], p[2], p[1]], axis=0)
    right = jnp.concatenate([q[0], q[1], q[0], q[2], q[0], q[1]], axis=0)
    return lax.dot_general(
        left.astype(jnp.bfloat16),
        right.astype(jnp.bfloat16),
        (((0,), (0,)), ((), ())),
        preferred_element_type=jnp.float32,
    )


def chunks_of(count):
    return max(n for n in range(1, CHUNKS + 1) if count // 128 % n == 0)


def split(x):
    high = x.astype(jnp.bfloat16)
    return high, (x - high.astype(jnp.float32)).astype(jnp.bfloat16)


def target_covariance(out, pos, strength, inverse_square, tile_layer, row_start, col_start):
    height, width = out.shape
    levels = strength.shape[0]

    def upright(axis):
        line = pos[pl.ds(axis, 1), pl.ds(row_start, height)]
        return jnp.broadcast_to(line, (TILE, height)).T

    rows = [upright(0), upright(1)]
    for i in range(height // TILE):
        for j in range(width // TILE):
            columns = pl.ds(pl.multiple_of(col_start + j * TILE, TILE), TILE)
            across = rows[0][i * TILE : (i + 1) * TILE] - pos[pl.ds(0, 1), columns]
            along = rows[1][i * TILE : (i + 1) * TILE] - pos[pl.ds(1, 1), columns]
            distance = across * across + along * along
            lowest = jnp.minimum(
                tile_layer[row_start // TILE + i], tile_layer[col_start // TILE + j]
            )

            def layer(l, total, distance=distance, lowest=lowest):
                weight = jnp.where(l <= lowest, strength[l], 0.0)
                return total + weight / (1.0 + distance * inverse_square[l])

            out[pl.ds(i * TILE, TILE), pl.ds(j * TILE, TILE)] = lax.fori_loop(
                0, levels, layer, jnp.zeros_like(distance)
            )


def gray_neighbours(c, n):
    position = c * 0
    after = c * 0
    before = c * 0
    ring = [i ^ (i >> 1) for i in range(n)]
    for i, node in enumerate(ring):
        position = jnp.where(c == node, i, position)
        after = jnp.where(c == node, ring[(i + 1) % n], after)
        before = jnp.where(c == node, ring[(i - 1) % n], before)
    return position, after, before


def pivots(t_ref, start, count):
    n = t_ref.shape[0]
    lanes = lax.broadcasted_iota(jnp.int32, (8, n), 1)
    wide = lax.broadcasted_iota(jnp.int32, (8, 2 * n), 1)
    down = lax.broadcasted_iota(jnp.int32, (8, 1), 0)

    def step(i, carry):
        k = pl.multiple_of(i * 8, 8)
        rows = t_ref[pl.ds(k, 8), :]
        left = rows[:, :n]
        columns = [
            jnp.sum(jnp.where(lanes == k + j, left, 0.0), axis=1, keepdims=True)
            for j in range(8)
        ]
        scale = jnp.ones((8, 1), jnp.float32)
        for j in range(8):
            pivot = columns[j][j : j + 1]
            scale = jnp.where(down == j, lax.rsqrt(pivot), scale)
            if j < 7:
                factor = jnp.where(down > j, columns[j] * (1.0 / pivot), 0.0)
                rows = rows - factor * rows[j : j + 1]
                for later in range(j + 1, 8):
                    columns[later] = columns[later] - factor * columns[later][j : j + 1]
        rows = rows * scale
        rows = jnp.where((wide >= n) | (wide >= k + down), rows, 0.0)
        below = jnp.where(lanes >= k + 8, rows[:, :n], 0.0)
        t_ref[...] = t_ref[...] - outer(below, rows)
        t_ref[pl.ds(k, 8), :] = rows
        return carry

    lax.fori_loop(start // 8, (start + count) // 8, step, 0)


def exchange_kernel(
    n_row,
    n_col,
    cov,
    targets,
    diag,
    pos,
    strength,
    inverse_square,
    tile_layer,
    row_raw,
    col_raw,
    head_raw,
    need_raw,
    factor_ref,
    inverse_ref,
    target_cov,
    blocks,
    t_ref,
    local_sem,
    diag_send,
    diag_recv,
    col_send,
    col_recv,
    row_send,
    row_recv,
    need_send,
    need_recv,
):
    r = lax.axis_index("row")
    c = lax.axis_index("col")
    row_count = row_raw.shape[0]
    col_count = col_raw.shape[1]
    width = head_raw.shape[1]
    need = need_raw.shape[1]
    col_chunks = chunks_of(col_count)
    even = lax.rem(r, 2) == 0
    place, after, before = gray_neighbours(c, n_col)
    far_row = jnp.minimum(r + 2, n_row - 1)
    near_row = jnp.where(even, r + 1, r - 1)

    head_copy = pltpu.make_async_copy(targets.at[pl.ds(0, PB), :], head_raw, local_sem.at[0])
    col_copy = pltpu.make_async_copy(cov.at[pl.ds(0, PB), :], col_raw, local_sem.at[1])
    row_copy = pltpu.make_async_copy(cov.at[:, pl.ds(0, PB)], row_raw, local_sem.at[2])
    pl.when(r == 0)(lambda: (head_copy.start(), col_copy.start(), None)[-1])
    pl.when(c == 0)(lambda: (row_copy.start(), None)[-1])

    barrier = pltpu.get_barrier_semaphore()
    for k in range(1, n_row):
        pl.semaphore_signal(
            barrier, inc=1, device_id=(c, lax.rem(r + k, n_row)), device_id_type=MESH
        )
    for k in range(1, n_col):
        pl.semaphore_signal(
            barrier, inc=1, device_id=(lax.rem(c + k, n_col), r), device_id_type=MESH
        )
    pl.semaphore_wait(barrier, n_row + n_col - 2)

    def remote(src, dst, send, recv, col, row):
        return pltpu.make_async_remote_copy(
            src_ref=src,
            dst_ref=dst,
            send_sem=send,
            recv_sem=recv,
            device_id=(col, row),
            device_id_type=MESH,
        )

    def chain(src, dst, send, recv):
        return (
            remote(src, dst, send.at[0], recv, c, far_row),
            remote(src, dst, send.at[1], recv, c, near_row),
        )

    def chain_start(copies, allowed):
        pl.when(allowed & even & (r + 2 < n_row))(lambda: (copies[0].start(), None)[-1])
        pl.when(allowed & even & (r + 1 < n_row))(lambda: (copies[1].start(), None)[-1])

    def chain_end(copies, allowed):
        pl.when(allowed & even & (r + 2 < n_row))(lambda: (copies[0].wait_send(), None)[-1])
        pl.when(allowed & even & (r + 1 < n_row))(lambda: (copies[1].wait_send(), None)[-1])

    quarters = [(0, 0), (HALF, 0), (HALF, HALF)]

    def diag_chain(i, source):
        dst = blocks.at[i]
        src = dst
        if source:
            src = diag.at[pl.ds(quarters[i][0], HALF), pl.ds(quarters[i][1], HALF)]
        return src, dst

    def diag_copies(i, source):
        src, dst = diag_chain(i, source)
        down = chain(src, dst, diag_send.at[i], diag_recv.at[i])
        across = [
            remote(src, dst, diag_send.at[i, 1 + k], diag_recv.at[i], k, r)
            for k in range(1, n_col)
        ]
        return down, across

    def diag_start(i, source, allowed):
        down, across = diag_copies(i, source)
        chain_start(down, allowed)
        for copy in across:
            pl.when(allowed)(lambda copy=copy: (copy.start(), None)[-1])

    def diag_wait(i):
        @pl.when((r > 0) | (c > 0))
        def _():
            diag_copies(i, False)[0][0].wait_recv()

    first = (r == 0) & (c == 0)
    for i in range(3):
        diag_start(i, True, first)

    chunk = col_count // col_chunks

    def col_copies(j, source):
        if j == 0:
            src = targets.at[pl.ds(0, PB), :] if source else head_raw
            return chain(src, head_raw, col_send.at[j], col_recv.at[j])
        columns = pl.ds((j - 1) * chunk, chunk)
        dst = col_raw.at[:, columns]
        src = cov.at[pl.ds(0, PB), columns] if source else dst
        return chain(src, dst, col_send.at[j], col_recv.at[j])

    def col_forward(j):
        @pl.when((r > 0) & even)
        def _():
            col_copies(j, False)[0].wait_recv()

        chain_start(col_copies(j, False), r > 0)

    target_covariance(
        target_cov,
        pos,
        strength,
        inverse_square,
        tile_layer,
        pl.multiple_of(r * need, 128),
        pl.multiple_of(c * width, 128),
    )

    for i in range(3):
        diag_wait(i)
        diag_start(i, False, (r > 0) & (c == 0))

    for j in range(col_chunks + 1):
        chain_start(col_copies(j, True), r == 0)

    step_rows = row_count // (2 * ROW_CHUNKS)

    def row_copies(j, way, source):
        rows = pl.ds((2 * j + way) * step_rows, step_rows)
        dst = row_raw.at[rows, :]
        src = cov.at[rows, pl.ds(0, PB)] if source else dst
        to = after if way == 0 else before
        return remote(src, dst, row_send.at[j, way], row_recv.at[j, way], to, r)

    def forwards(way):
        return (place > 0) & ((place < n_col - 1) if way == 0 else (place > 1))

    def row_forward(j):
        for way in range(2):
            copy = row_copies(j, way, False)
            pl.when(forwards(way))(lambda copy=copy: (copy.wait_recv(), copy.start(), None)[-1])

    for j in range(ROW_CHUNKS):
        for way in range(2):
            copy = row_copies(j, way, True)
            pl.when(place == 0)(lambda copy=copy: (copy.start(), None)[-1])

    owner = lax.div(r * need, width)
    offset = pl.multiple_of(lax.rem(r * need, width), 128)
    need_copies = [
        remote(
            head_raw.at[:, pl.ds(offset, need)], need_raw, need_send.at[k], need_recv, k, r
        )
        for k in range(n_col)
    ]
    own_need = pltpu.make_async_copy(
        head_raw.at[:, pl.ds(offset, need)], need_raw, local_sem.at[3]
    )

    def need_start():
        pl.when(r == 0)(lambda: (head_copy.wait(), None)[-1])
        pl.when((r > 0) & ~even & (c == owner))(
            lambda: (col_copies(0, False)[0].wait_recv(), None)[-1]
        )
        for k in range(n_col):
            pl.when((c == owner) & (c != k))(lambda k=k: (need_copies[k].start(), None)[-1])
        pl.when(c == owner)(lambda: (own_need.start(), None)[-1])

    @pl.when(first)
    def _():
        for i in range(3):
            blocks[i] = diag[pl.ds(quarters[i][0], HALF), pl.ds(quarters[i][1], HALF)]

    unit = (
        lax.broadcasted_iota(jnp.int32, (HALF, HALF), 0)
        == lax.broadcasted_iota(jnp.int32, (HALF, HALF), 1)
    ).astype(jnp.float32)
    events = [lambda: row_forward(0), lambda: (col_forward(0), need_start(), row_forward(1))]
    for j in range(max(col_chunks, ROW_CHUNKS)):
        if j + 2 < ROW_CHUNKS:
            events.append(lambda j=j: row_forward(j + 2))
        if j < col_chunks:
            events.append(lambda j=j: col_forward(j + 1))

    def half(block, where):
        t_ref[:, pl.ds(0, HALF)] = block
        t_ref[:, pl.ds(HALF, HALF)] = unit
        for start in range(0, HALF, SEGMENT):
            pivots(t_ref, start, SEGMENT)
            if events:
                events.pop(0)()

    half(blocks[0], 0)
    inverse_11 = t_ref[:, pl.ds(HALF, HALF)]
    inverse_ref[pl.ds(0, HALF), pl.ds(0, HALF)] = inverse_11
    inverse_ref[pl.ds(0, HALF), pl.ds(HALF, HALF)] = jnp.zeros((HALF, HALF), jnp.float32)
    factor_ref[pl.ds(0, HALF), pl.ds(0, HALF)] = t_ref[:, pl.ds(0, HALF)].T
    factor_ref[pl.ds(0, HALF), pl.ds(HALF, HALF)] = jnp.zeros((HALF, HALF), jnp.float32)
    lower = dot(blocks[1], inverse_11, ((1,), (1,)))
    factor_ref[pl.ds(HALF, HALF), pl.ds(0, HALF)] = lower
    half(blocks[2] - dot(lower, lower, ((1,), (1,))), 1)
    inverse_22 = t_ref[:, pl.ds(HALF, HALF)]
    inverse_ref[pl.ds(HALF, HALF), pl.ds(HALF, HALF)] = inverse_22
    factor_ref[pl.ds(HALF, HALF), pl.ds(HALF, HALF)] = t_ref[:, pl.ds(0, HALF)].T
    lower = factor_ref[pl.ds(HALF, HALF), pl.ds(0, HALF)]
    inverse_ref[pl.ds(HALF, HALF), pl.ds(0, HALF)] = -dot(
        inverse_22, dot(lower, inverse_ref[pl.ds(0, HALF), pl.ds(0, HALF)])
    )
    while events:
        events.pop(0)()

    for j in range(col_chunks + 1):
        late = ~even & (c != owner) if j == 0 else ~even
        pl.when(late)(lambda j=j: (col_copies(j, False)[0].wait_recv(), None)[-1])
    for j in range(ROW_CHUNKS):
        for way in range(2):
            copy = row_copies(j, way, False)
            pl.when((place > 0) & ~forwards(way))(lambda copy=copy: (copy.wait_recv(), None)[-1])
    pl.when(c == owner)(lambda: (own_need.wait(), None)[-1])
    pl.when(c != owner)(lambda: (need_copies[0].wait_recv(), None)[-1])
    for k in range(n_col):
        pl.when((c == owner) & (c != k))(lambda k=k: (need_copies[k].wait_send(), None)[-1])
    for i in range(3):
        down, across = diag_copies(i, True)
        chain_end(down, c == 0)
        for copy in across:
            pl.when(c == 0)(lambda copy=copy: (copy.wait_send(), None)[-1])
    for j in range(col_chunks + 1):
        chain_end(col_copies(j, False), r >= 0)
    for j in range(ROW_CHUNKS):
        for way in range(2):
            copy = row_copies(j, way, False)
            pl.when((place == 0) | forwards(way))(lambda copy=copy: (copy.wait_send(), None)[-1])
    pl.when(r == 0)(lambda: (col_copy.wait(), None)[-1])
    pl.when(c == 0)(lambda: (row_copy.wait(), None)[-1])


def update_kernel(
    cov,
    row_raw,
    targets,
    noise,
    col_raw,
    head_raw,
    need_raw,
    factor,
    inverse,
    target_cov,
    updated,
    panel,
    reconstructor,
    error_cov,
    left,
    left_parts,
    head,
    head_parts,
):
    t = pl.program_id(0)
    r = lax.axis_index("row")
    c = lax.axis_index("col")
    rows, cols = cov.shape
    part = panel.shape[0]

    @pl.when(t == 0)
    def _():
        whole = inverse[...]
        solved = dot(row_raw[...], whole, ((1,), (1,)))
        left[...] = solved
        high, low = split(solved)
        left_parts[:, pl.ds(0, PB)] = high
        left_parts[:, pl.ds(PB, PB)] = low
        left_parts[:, pl.ds(2 * PB, PB)] = high

        @pl.when(r == 0)
        def _():
            left[pl.ds(0, PB), :] = factor[...]

        solved = dot(whole, head_raw[...])
        head[...] = solved
        high, low = split(solved)
        head_parts[...] = jnp.concatenate([high, high, low], axis=0)
        other = dot(whole, need_raw[...])
        error_cov[...] = target_cov[...] - dot(other, solved, ((0,), (0,)))

    here = pl.ds(pl.multiple_of(t * part, part), part)
    panel[...] = left[here, :]
    reconstructor[...] = targets[...] - jnp.dot(
        left_parts[here, :], head_parts[...], preferred_element_type=jnp.float32
    )

    @pl.when((r == 0) & (t < PB // part))
    def _():
        block = pl.ds(pl.multiple_of(jnp.minimum(t, PB // part - 1) * part, part), part)
        reconstructor[...] = head[block, :]

    high, low = split(dot(inverse[...], col_raw[...]))
    updated[...] = cov[...] - jnp.dot(
        left_parts[...],
        jnp.concatenate([high, high, low], axis=0),
        preferred_element_type=jnp.float32,
    )
    start = c * (cols * pl.num_programs(0)) + t * cols - r * rows

    @pl.when((start >= 0) & (start < rows))
    def _():
        block = pl.ds(pl.multiple_of(start, cols), cols)
        diagonal = lax.broadcasted_iota(jnp.int32, (cols, cols), 0) == (
            lax.broadcasted_iota(jnp.int32, (cols, cols), 1)
        )
        updated[block, :] = updated[block, :] + jnp.where(diagonal, noise[start // cols], 0.0)

    @pl.when(r == 0)
    def _():
        updated[pl.ds(0, PB), :] = jnp.zeros((PB, cols), jnp.float32)

    @pl.when((c == 0) & (t == 0))
    def _():
        updated[...] = left[...]


def local(
    n_row, n_col, covariance, wfs_map, noise_var, targets, target_pos, layer_strength,
    layer_scale, tile_layer
):
    row_count, col_count = covariance.shape
    target_width = targets.shape[1]
    kinds = jnp.arange(noise_var.shape[0], dtype=jnp.int32)
    noise_rows = jnp.sum(
        jnp.where(wfs_map[None, :] == kinds[:, None], noise_var[:, None], 0.0), axis=0
    )
    diag = covariance[:PB, :PB] + jnp.where(
        jnp.arange(PB)[:, None] == jnp.arange(PB)[None, :], noise_rows[None, :PB], 0.0
    )
    error_rows = target_width * n_col // n_row
    col_chunks = chunks_of(col_count)
    def f32(*shape):
        return jax.ShapeDtypeStruct(shape, jnp.float32)

    vmem = pl.BlockSpec(memory_space=pltpu.VMEM)
    anywhere = pl.BlockSpec(memory_space=pltpu.HBM)
    smem = pl.BlockSpec(memory_space=pltpu.SMEM)
    dma = pltpu.SemaphoreType.DMA
    row_raw, col_raw, head_raw, need_raw, factor, inverse, target_cov = pl.pallas_call(
        functools.partial(exchange_kernel, n_row, n_col),
        out_shape=(
            f32(row_count, PB),
            f32(PB, col_count),
            f32(PB, target_width),
            f32(PB, error_rows),
            f32(PB, PB),
            f32(PB, PB),
            f32(error_rows, target_width),
        ),
        in_specs=[anywhere, anywhere, vmem, vmem, smem, smem, smem],
        out_specs=[vmem] * 7,
        scratch_shapes=[
            pltpu.VMEM((3, HALF, HALF), jnp.float32),
            pltpu.VMEM((HALF, PB), jnp.float32),
            dma((4,)),
            dma((3, n_col + 1)),
            dma((3,)),
            dma((col_chunks + 1, 2)),
            dma((col_chunks + 1,)),
            dma((ROW_CHUNKS, 2)),
            dma((ROW_CHUNKS, 2)),
            dma((n_col,)),
            dma,
        ],
        compiler_params=pltpu.CompilerParams(
            collective_id=0, has_side_effects=True, vmem_limit_bytes=46 * 1024 * 1024
        ),
        name="exchange",
    )(
        covariance,
        targets,
        diag,
        target_pos,
        layer_strength,
        1.0 / (layer_scale * layer_scale),
        tile_layer,
    )

    steps = col_count // PB
    part = row_count // steps

    def tiled(width):
        return pl.BlockSpec((part, width), lambda t: (t, 0))

    def across(height):
        return pl.BlockSpec((height, PB), lambda t: (0, t))

    def held(height, width):
        return pl.BlockSpec((height, width), lambda t: (0, 0))

    return pl.pallas_call(
        update_kernel,
        grid=(steps,),
        out_shape=(
            f32(row_count, col_count),
            f32(row_count, PB),
            f32(row_count, target_width),
            f32(error_rows, target_width),
        ),
        in_specs=[
            across(row_count),
            held(row_count, PB),
            tiled(target_width),
            pl.BlockSpec((row_count // PB, 1, PB), lambda t: (0, 0, 0)),
            across(PB),
            held(PB, target_width),
            held(PB, error_rows),
            held(PB, PB),
            held(PB, PB),
            held(error_rows, target_width),
        ],
        out_specs=[
            across(row_count),
            tiled(PB),
            tiled(target_width),
            held(error_rows, target_width),
        ],
        scratch_shapes=[
            pltpu.VMEM((row_count, PB), jnp.float32),
            pltpu.VMEM((row_count, 3 * PB), jnp.bfloat16),
            pltpu.VMEM((PB, target_width), jnp.float32),
            pltpu.VMEM((3 * PB, target_width), jnp.bfloat16),
        ],
        compiler_params=pltpu.CompilerParams(vmem_limit_bytes=40 * 1024 * 1024),
        name="update",
    )(
        covariance,
        row_raw,
        targets,
        noise_rows.reshape(row_count // PB, 1, PB),
        col_raw,
        head_raw,
        need_raw,
        factor,
        inverse,
        target_cov,
    )


def solution(mesh):
    placed = (P("row", "col"), P("row"), P(), P("row", "col"), P(), P(), P(), P())
    return jax.shard_map(
        functools.partial(local, mesh.shape["row"], mesh.shape["col"]),
        mesh=mesh,
        in_specs=placed,
        out_specs=(P("row", "col"), P("row", None), P("row", "col"), P("row", "col")),
        check_vma=False,
    )
```

profile of v0, /device:TPU:31, one launch (start us, length us, event | category | flops | bytes accessed | tf_op | source)
XLA Modules:
  0.0 119.7 jit_solution(11428148852253734647)
XLA Ops:
  0.6 0.7 multiply_divide_fusion.inverse_square
  1.3 0.8 select_reduce_fusion
  2.1 1.0 select_add_fusion.diag
  3.1 0.0 copy-start.1
  3.1 0.7 copy-done.1
  3.8 0.0 copy-start.2
  3.8 0.7 copy-done.2
  4.5 0.0 copy-start.3
  4.5 0.7 copy-done.3
  5.1 0.0 copy-start
  5.1 83.3 %exchange.1 = (f32[1536,256]{1,0:T(8,128)S(1)}, f32[256,3072]{1,0:T(8,128)S(1)}, f32[256,512]{1,0:T(8,128)S(1)}, f32[256,256]{1,0:T(8,128)S(1)}, f32[256,256]{1,...) custom-call(f32[1536,3072]{1,0:T(8,128)} %cov.3, f32[1536,512]{1,0:T(8,128)} %targets.3, ...), custom_call_target="tpu_custom_call" | custom-call | tf_op jit(solution)/shard_map/exchange/pallas_call | solution.py:493
  88.5 0.0 copy-done
  88.5 31.3 %update.1 = (f32[1536,3072]{1,0:T(8,128)}, f32[1536,256]{1,0:T(8,128)}, f32[1536,512]{1,0:T(8,128)}, f32[256,512]{1,0:T(8,128)}) custom-call(f32[1536,3072]{1,0:T(8,128)} %cov.3, f32[1536,256]{1,0:T(8,128)S(1)} %get-tuple-element.11.row_raw, f32[1536,512]{1,0:T(8,128)S(1)} %copy-done, f32[6,1,256]{2,1,0:T(1,128)S(1)} %reshape.14.noise, ...), custom_call_target="tpu_custom_call" | custom-call | tf_op jit(solution)/shard_map/update/pallas_call | solution.py:545
  (2 shorter events, 0.0 us)
Async XLA Ops:
  3.1 0.7 copy-start.1
  3.8 0.7 copy-start.2
  4.5 0.7 copy-start.3
  5.1 83.3 %copy-start = (f32[1536,512]{1,0:T(8,128)S(1)}, f32[1536,512]{1,0:T(8,128)}, u32[]{:S(2)}) copy-start(f32[1536,512]{1,0:T(8,128)} %targets.3) | copy-start | bytes 9437188
where the time goes:
time: 121 us; the launch traced here: 120 us
  Pallas kernels  115 us (95%)
  other arithmetic  2.44 us (2%)
  local copies, waits for them, and re-layouts  2.04 us (2%)
    pallas_call x1, Pallas kernels, local(): pl.pallas_call(functools.partial(exchange_kernel, n_row, n_col), out_shap...  83.3 us
    pallas_call x1, Pallas kernels, local(): pl.pallas_call(update_kernel, grid=(steps,), out_shape=(f32(row_count, co...  31.3 us

commit v1 on v0

v1 whole, which is shorter than its diff:
```python
import functools

import jax
import jax.numpy as jnp
from jax import lax
from jax.experimental import pallas as pl
from jax.experimental.pallas import tpu as pltpu
from jax.sharding import PartitionSpec as P

PB = 256
TILE = 128
HALF = PB // 2
STEP = 8
CHUNK = 128
ROW_CHUNKS = 12
AHEAD = 2
LATE = 2

MESH = pl.DeviceIdType.MESH
precise = lax.Precision.HIGHEST


def dot(a, b, dims=((1,), (0,))):
    return lax.dot_general(
        a, b, (dims, ((), ())), precision=precise, preferred_element_type=jnp.float32
    )


def outer(a, b):
    def thirds(x):
        high = x.astype(jnp.bfloat16).astype(jnp.float32)
        middle = (x - high).astype(jnp.bfloat16).astype(jnp.float32)
        return high, middle, x - high - middle

    p, q = thirds(a), thirds(b)
    left = jnp.concatenate([p[0], p[0], p[1], p[0], p[2], p[1]], axis=0)
    right = jnp.concatenate([q[0], q[1], q[0], q[2], q[0], q[1]], axis=0)
    return lax.dot_general(
        left.astype(jnp.bfloat16),
        right.astype(jnp.bfloat16),
        (((0,), (0,)), ((), ())),
        preferred_element_type=jnp.float32,
    )


def split(x):
    high = x.astype(jnp.bfloat16)
    return high, (x - high.astype(jnp.float32)).astype(jnp.bfloat16)


def stacked(x):
    high, low = split(x)
    return jnp.concatenate([high, high, low], axis=0)


def target_covariance(out, product, pos, strength, scale, tile_layer, row_start, col_start):
    height, width = out.shape

    def upright(axis):
        line = pos[pl.ds(axis, 1), pl.ds(row_start, height)]
        return jnp.broadcast_to(line, (TILE, height)).T

    rows = [upright(0), upright(1)]
    for i in range(height // TILE):
        for j in range(width // TILE):
            columns = pl.ds(pl.multiple_of(col_start + j * TILE, TILE), TILE)
            across = rows[0][i * TILE : (i + 1) * TILE] - pos[pl.ds(0, 1), columns]
            along = rows[1][i * TILE : (i + 1) * TILE] - pos[pl.ds(1, 1), columns]
            distance = across * across + along * along
            lowest = jnp.minimum(
                tile_layer[row_start // TILE + i], tile_layer[col_start // TILE + j]
            )

            def layer(l, total, distance=distance):
                return total + strength[l] / (1.0 + distance * (1.0 / (scale[l] * scale[l])))

            total = lax.fori_loop(0, lowest + 1, layer, jnp.zeros_like(distance))
            here = (pl.ds(i * TILE, TILE), pl.ds(j * TILE, TILE))
            out[here] = total - product[here]


def gray_neighbours(c, n):
    position = c * 0
    after = c * 0
    before = c * 0
    ring = [i ^ (i >> 1) for i in range(n)]
    for i, node in enumerate(ring):
        position = jnp.where(c == node, i, position)
        after = jnp.where(c == node, ring[(i + 1) % n], after)
        before = jnp.where(c == node, ring[(i - 1) % n], before)
    return position, after, before


def pivot_step(t_ref, i):
    n = t_ref.shape[0]
    lanes = lax.broadcasted_iota(jnp.int32, (8, n), 1)
    wide = lax.broadcasted_iota(jnp.int32, (8, 2 * n), 1)
    down = lax.broadcasted_iota(jnp.int32, (8, 1), 0)
    k = pl.multiple_of(i * 8, 8)
    rows = t_ref[pl.ds(k, 8), :]
    left = rows[:, :n]
    columns = [
        jnp.sum(jnp.where(lanes == k + j, left, 0.0), axis=1, keepdims=True) for j in range(8)
    ]
    scale = jnp.ones((8, 1), jnp.float32)
    for j in range(8):
        pivot = columns[j][j : j + 1]
        scale = jnp.where(down == j, lax.rsqrt(pivot), scale)
        if j < 7:
            factor = jnp.where(down > j, columns[j] * (1.0 / pivot), 0.0)
            rows = rows - factor * rows[j : j + 1]
            for later in range(j + 1, 8):
                columns[later] = columns[later] - factor * columns[later][j : j + 1]
    rows = rows * scale
    rows = jnp.where((wide >= n) | (wide >= k + down), rows, 0.0)
    below = jnp.where(lanes >= k + 8, rows[:, :n], 0.0)
    t_ref[...] = t_ref[...] - outer(below, rows)
    t_ref[pl.ds(k, 8), :] = rows


def run(condition, action):
    @pl.when(condition)
    def _():
        action()


def panel_kernel(
    n_row,
    n_col,
    cov,
    targets,
    sensors,
    noise_var,
    updated,
    reconstructor,
    panel,
    product,
    row_raw,
    col_raw,
    need_raw,
    blocks,
    head_sensors,
    own_sensors,
    kinds,
    noise,
    t_ref,
    factor_ref,
    inverse_ref,
    parts,
    solver,
    local_sem,
    cov_sem,
    diag_send,
    diag_recv,
    col_send,
    col_recv,
    row_send,
    row_recv,
    need_send,
    need_recv,
):
    r = lax.axis_index("row")
    c = lax.axis_index("col")
    row_count, col_count = updated.shape
    width = reconstructor.shape[1]
    need = need_raw.shape[1]
    pairs = col_count // PB
    head_chunks = width // CHUNK
    chunks = head_chunks + col_count // CHUNK
    even = lax.rem(r, 2) == 0
    plane = lax.div(r, 2)
    place, after, before = gray_neighbours(c, n_col)
    far_row = jnp.minimum(r + 2, n_row - 1)
    near_row = jnp.where(even, r + 1, r - 1)
    has_far = even & (r + 2 < n_row)
    has_near = even & (r + 1 < n_row)
    relays = even & (r > 0)
    first = (r == 0) & (c == 0)
    half_ring = n_col // 2

    head_span = pl.ds(0, width)
    head_copy = pltpu.make_async_copy(
        targets.at[pl.ds(0, PB), :], col_raw.at[:, head_span], local_sem.at[0]
    )
    col_copy = pltpu.make_async_copy(
        cov.at[pl.ds(0, PB), :], col_raw.at[:, pl.ds(width, col_count)], local_sem.at[1]
    )
    row_copy = pltpu.make_async_copy(cov.at[:, pl.ds(0, PB)], row_raw, local_sem.at[2])
    target_copy = pltpu.make_async_copy(targets, reconstructor, local_sem.at[3])
    sensor_copy = pltpu.make_async_copy(sensors, own_sensors, local_sem.at[9])
    noise_copy = pltpu.make_async_copy(noise_var, kinds, local_sem.at[10])
    quarters = [(0, 0), (HALF, 0), (HALF, HALF)]

    def diag_piece(i, source):
        if i == 0:
            return (sensors.at[pl.ds(0, PB)] if source else head_sensors), head_sensors
        dst = blocks.at[i - 1]
        if source:
            y, x = quarters[i - 1]
            return cov.at[pl.ds(y, HALF), pl.ds(x, HALF)], dst
        return dst, dst

    own_diag = [
        pltpu.make_async_copy(*diag_piece(i, True), local_sem.at[5 + i]) for i in range(4)
    ]

    def cov_copy(p):
        columns = pl.ds(pl.multiple_of(p * PB, PB), PB)
        return pltpu.make_async_copy(cov.at[:, columns], updated.at[:, columns], cov_sem.at[p])

    for copy in own_diag:
        run(first, copy.start)
    sensor_copy.start()
    noise_copy.start()

    barrier = pltpu.get_barrier_semaphore()

    def greet(col, row):
        pl.semaphore_signal(barrier, inc=1, device_id=(col, row), device_id_type=MESH)

    greet(c, near_row)
    for k in range(1, n_col):
        greet(lax.rem(c + k, n_col), r)
    run(has_far, lambda: greet(c, far_row))
    run(relays, lambda: greet(c, jnp.maximum(r - 2, 0)))
    pl.semaphore_wait(barrier, n_col + jnp.where(has_far, 1, 0) + jnp.where(relays, 1, 0))

    def remote(src, dst, send, recv, col, row):
        return pltpu.make_async_remote_copy(
            src_ref=src,
            dst_ref=dst,
            send_sem=send,
            recv_sem=recv,
            device_id=(col, row),
            device_id_type=MESH,
        )

    def upward(src, dst, send, recv):
        return (
            remote(src, dst, send[0], recv, c, far_row),
            remote(src, dst, send[1], recv, c, near_row),
        )

    def diag_copies(i, source):
        src, dst = diag_piece(i, source)
        ring = [
            remote(src, dst, diag_send.at[i, k], diag_recv.at[i], to, r)
            for k, to in enumerate([after, before])
        ]
        return ring, upward(src, dst, [diag_send.at[i, 2], diag_send.at[i, 3]], diag_recv.at[i])

    ring_after = (r == 0) & (place < half_ring)
    ring_before = (r == 0) & ((place == 0) | (place >= half_ring + 2))

    def diag_each(i, source, allowed, what):
        ring, up = diag_copies(i, source)
        run(allowed & has_far, lambda: what(up[0]))
        run(allowed & has_near, lambda: what(up[1]))
        run(allowed & ring_after, lambda: what(ring[0]))
        run(allowed & ring_before, lambda: what(ring[1]))

    def start(copy):
        copy.start()

    def finish(copy):
        copy.wait_send()

    def span(q):
        return pl.ds(pl.multiple_of(q * CHUNK, CHUNK), CHUNK)

    def chunk_copies(q, src):
        return upward(
            src, col_raw.at[:, span(q)], [col_send.at[q, 0], col_send.at[q, 1]], col_recv.at[q]
        )

    def chunk_start(copies):
        run(has_far, copies[0].start)
        run(has_near, copies[1].start)

    def source_chunk(q):
        run(
            q < head_chunks,
            lambda: chunk_start(
                chunk_copies(q, targets.at[pl.ds(0, PB), span(jnp.minimum(q, head_chunks - 1))])
            ),
        )
        run(
            q >= head_chunks,
            lambda: chunk_start(
                chunk_copies(q, cov.at[pl.ds(0, PB), span(jnp.maximum(q - head_chunks, 0))])
            ),
        )

    def each(low, high, action):
        def body(i, carry):
            action(i)
            return carry

        lax.fori_loop(low, high, body, 0)

    def chunk_take(q):
        copies = chunk_copies(q, col_raw.at[:, span(q)])
        copies[0].wait_recv()
        run(even, lambda: chunk_start(copies))

    def takes(low, high):
        run(relays, lambda: each(low, high, chunk_take))

    step_rows = row_count // (2 * ROW_CHUNKS)

    def row_copies(j, way, source):
        rows = pl.ds(pl.multiple_of((2 * j + way) * step_rows, step_rows), step_rows)
        dst = row_raw.at[rows, :]
        src = cov.at[rows, pl.ds(0, PB)] if source else dst
        to = after if way == 0 else before
        return remote(src, dst, row_send.at[j, way], row_recv.at[j, way], to, r)

    def forwards(way):
        return (place > 0) & ((place < n_col - 1) if way == 0 else (place > 1))

    def row_source(j):
        for way in range(2):
            row_copies(j, way, True).start()

    def row_forward(j):
        for way in range(2):
            copy = row_copies(j, way, False)
            run(forwards(way), lambda: (copy.wait_recv(), copy.start()))

    def diag_pass(i):
        run((r > 0) | (c > 0), diag_copies(i, False)[0][0].wait_recv)
        diag_each(i, False, ~first, start)
        run(first, own_diag[i].wait)

    def noise_of(sensor):
        total = jnp.zeros(sensor.shape, jnp.float32)
        for k in range(noise_var.shape[0]):
            total = jnp.where(sensor == k, kinds[k], total)
        return total

    def row_goal(s):
        late = jnp.where(place == half_ring, 7, 2) + jnp.where(plane == 0, 3, 0)
        return jnp.clip(lax.div(jnp.maximum(s + 4 * plane - late, 0), 3), 0, ROW_CHUNKS)

    for i in range(4):
        diag_each(i, True, first, start)
    run((r == 0) & (c > 0), lambda: each(0, AHEAD, source_chunk))
    run((place == 0) & ((r == 0) | (r > 1)), lambda: each(0, ROW_CHUNKS, row_source))
    run(first, lambda: each(0, chunks, source_chunk))
    run(c > 0, lambda: takes(0, AHEAD))
    each(0, row_goal(-1), row_forward)
    diag_pass(0)
    diag_pass(1)
    sensor_copy.wait()
    noise_copy.wait()
    noise[...] = noise_of(own_sensors[...].reshape(1, row_count))
    head_noise = noise_of(head_sensors[...].reshape(1, PB))
    unit = lax.broadcasted_iota(jnp.int32, (HALF, HALF), 0) == lax.broadcasted_iota(
        jnp.int32, (HALF, HALF), 1
    )

    def chunk_goal(s):
        late = jnp.where(c == 0, 5, 1)
        return jnp.maximum(lax.div(jnp.maximum(s - late, 0), 3), jnp.where(c == 0, 0, AHEAD))

    steps = HALF // STEP

    def side_work(s):
        @pl.when(s == 2)
        def _():
            diag_pass(2)

        @pl.when(s == 4)
        def _():
            diag_pass(3)
            run((place == 0) & (r == 1), lambda: each(0, ROW_CHUNKS, row_source))
            run((r == 0) & (c > 0), lambda: each(AHEAD, chunks, source_chunk))

        @pl.when(s == 6)
        def _():
            run(r == 0, lambda: (head_copy.start(), col_copy.start()))
            run(c == 0, row_copy.start)

        run(s == 8, target_copy.start)
        run((lax.rem(s, 2) == 1) & (lax.div(s, 2) < pairs), lambda: cov_copy(lax.div(s, 2)).start())
        takes(chunk_goal(s - 1), chunk_goal(s))
        each(row_goal(s - 1), row_goal(s), row_forward)

    def half(block, where):
        t_ref[:, pl.ds(0, HALF)] = block
        t_ref[:, pl.ds(HALF, HALF)] = unit.astype(jnp.float32)

        def step(i, carry):
            pivot_step(t_ref, i)
            side_work(i + where * steps)
            return carry

        lax.fori_loop(0, steps, step, 0)

    owner = lax.div(r * need, width)
    offset = pl.multiple_of(lax.rem(r * need, width), CHUNK)
    need_copies = [
        remote(col_raw.at[:, pl.ds(offset, need)], need_raw, need_send.at[k], need_recv, k, r)
        for k in range(n_col)
    ]
    own_need = pltpu.make_async_copy(
        col_raw.at[:, pl.ds(offset, need)], need_raw, local_sem.at[4]
    )

    def need_start():
        run(r == 0, head_copy.wait)
        run(~even, lambda: each(0, head_chunks, chunk_take))
        for k in range(n_col):
            run((c == owner) & (c != k), need_copies[k].start)
        run(c == owner, own_need.start)

    half(blocks[0] + jnp.where(unit, head_noise[:, :HALF], 0.0), 0)
    inverse_11 = t_ref[:, pl.ds(HALF, HALF)]
    inverse_ref[pl.ds(0, HALF), pl.ds(0, HALF)] = inverse_11
    inverse_ref[pl.ds(0, HALF), pl.ds(HALF, HALF)] = jnp.zeros((HALF, HALF), jnp.float32)
    factor_ref[pl.ds(0, HALF), pl.ds(0, HALF)] = t_ref[:, pl.ds(0, HALF)].T
    factor_ref[pl.ds(0, HALF), pl.ds(HALF, HALF)] = jnp.zeros((HALF, HALF), jnp.float32)
    lower = dot(blocks[1], inverse_11, ((1,), (1,)))
    factor_ref[pl.ds(HALF, HALF), pl.ds(0, HALF)] = lower
    half(
        blocks[2]
        + jnp.where(unit, head_noise[:, HALF:], 0.0)
        - dot(lower, lower, ((1,), (1,))),
        1,
    )
    inverse_22 = t_ref[:, pl.ds(HALF, HALF)]
    inverse_ref[pl.ds(HALF, HALF), pl.ds(HALF, HALF)] = inverse_22
    factor_ref[pl.ds(HALF, HALF), pl.ds(HALF, HALF)] = t_ref[:, pl.ds(0, HALF)].T
    lower = factor_ref[pl.ds(HALF, HALF), pl.ds(0, HALF)]
    inverse_ref[pl.ds(HALF, HALF), pl.ds(0, HALF)] = -dot(
        inverse_22, dot(lower, inverse_ref[pl.ds(0, HALF), pl.ds(0, HALF)])
    )
    last = 2 * steps - 1
    each(row_goal(last), ROW_CHUNKS, row_forward)
    goal = chunk_goal(last)
    takes(goal, goal + LATE)
    goal = goal + LATE

    inverse = inverse_ref[...]
    solver[:, pl.ds(0, PB)] = stacked(inverse.T)
    solver[:, pl.ds(PB, PB)] = stacked(dot(inverse, inverse, ((0,), (0,))))

    def row_wait(j):
        for way in range(2):
            run((place > 0) & ~forwards(way), row_copies(j, way, False).wait_recv)

    each(0, ROW_CHUNKS, row_wait)
    run(c == 0, row_copy.wait)
    takes(goal, goal + 1)
    goal = goal + 1
    need_start()
    each(min(2 * steps // 2, pairs), pairs, lambda p: cov_copy(p).start())

    def solve(i, carry):
        rows = pl.ds(pl.multiple_of(i * PB, PB), PB)
        high, low = split(row_raw[rows, :])
        both = jnp.dot(
            jnp.concatenate([high, low, high], axis=1),
            solver[...],
            preferred_element_type=jnp.float32,
        )
        panel[rows, :] = both[:, :PB]
        high, low = split(both[:, PB:])
        parts[rows, pl.ds(0, PB)] = high
        parts[rows, pl.ds(PB, PB)] = low
        parts[rows, pl.ds(2 * PB, PB)] = high
        return carry

    lax.fori_loop(0, row_count // PB, solve, 0)

    @pl.when(r == 0)
    def _():
        panel[pl.ds(0, PB), :] = factor_ref[...]

    takes(goal, goal + 1)
    goal = goal + 1

    head = dot(inverse, col_raw[:, head_span])
    target_copy.wait()
    reconstructor[...] = reconstructor[...] - jnp.dot(
        parts[...], stacked(col_raw[:, head_span]), preferred_element_type=jnp.float32
    )

    @pl.when(r == 0)
    def _():
        reconstructor[pl.ds(0, PB), :] = head

    run(r == 0, col_copy.wait)

    def reach(p):
        return jnp.minimum(jnp.maximum(goal + p, head_chunks + 2 * p), chunks)

    def update(p):
        takes(reach(p), reach(p + 1))
        run(
            ~even,
            lambda: each(head_chunks + 2 * p, head_chunks + 2 * p + 2, chunk_take),
        )
        cov_copy(p).wait()
        columns = pl.ds(pl.multiple_of(p * PB, PB), PB)
        raw = col_raw[:, pl.ds(pl.multiple_of(width + p * PB, CHUNK), PB)]
        updated[:, columns] = updated[:, columns] - jnp.dot(
            parts[...], stacked(raw), preferred_element_type=jnp.float32
        )
        begin = c * col_count + p * PB - r * row_count

        @pl.when((begin >= 0) & (begin < row_count))
        def _():
            block = pl.ds(pl.multiple_of(begin, PB), PB)
            diagonal = lax.broadcasted_iota(jnp.int32, (PB, PB), 0) == (
                lax.broadcasted_iota(jnp.int32, (PB, PB), 1)
            )
            updated[block, columns] = updated[block, columns] + jnp.where(
                diagonal, noise[:, block], 0.0
            )

        @pl.when(r == 0)
        def _():
            updated[pl.ds(0, PB), columns] = jnp.zeros((PB, PB), jnp.float32)

    def finish_product():
        run(c == owner, own_need.wait)
        run(c != owner, need_copies[0].wait_recv)
        product[...] = dot(dot(inverse, need_raw[...]), head, ((0,), (0,)))

    tail = pairs - pairs // 6
    each(0, tail, update)
    finish_product()
    each(tail, pairs, update)

    @pl.when(c == 0)
    def _():
        updated[:, pl.ds(0, PB)] = panel[...]

    for k in range(n_col):
        run((c == owner) & (c != k), need_copies[k].wait_send)
    for i in range(4):
        diag_each(i, False, r >= 0, finish)

    def chunk_finish(q):
        copies = chunk_copies(q, col_raw.at[:, span(q)])
        run(has_far, copies[0].wait_send)
        run(has_near, copies[1].wait_send)

    each(0, chunks, chunk_finish)

    def row_finish(j):
        for way in range(2):
            run((place == 0) | forwards(way), row_copies(j, way, False).wait_send)

    each(0, ROW_CHUNKS, row_finish)


SLABS = 6


def store_kernel(
    updated,
    reconstructor,
    panel,
    product,
    pos,
    strength,
    scale,
    tile_layer,
    updated_out,
    reconstructor_out,
    panel_out,
    error_out,
    error,
    sems,
):
    r = lax.axis_index("row")
    c = lax.axis_index("col")
    slab = updated.shape[0] // SLABS
    copies = [
        pltpu.make_async_copy(
            updated.at[pl.ds(i * slab, slab), :],
            updated_out.at[pl.ds(i * slab, slab), :],
            sems.at[i],
        )
        for i in range(SLABS)
    ]
    copies.append(pltpu.make_async_copy(reconstructor, reconstructor_out, sems.at[SLABS]))
    copies.append(pltpu.make_async_copy(panel, panel_out, sems.at[SLABS + 1]))
    for copy in copies:
        copy.start()
    height, width = error.shape
    target_covariance(
        error,
        product,
        pos,
        strength,
        scale,
        tile_layer,
        pl.multiple_of(r * height, TILE),
        pl.multiple_of(c * width, TILE),
    )
    last = pltpu.make_async_copy(error, error_out, sems.at[SLABS + 2])
    last.start()
    for copy in copies:
        copy.wait()
    last.wait()


def local(
    n_row, n_col, covariance, wfs_map, noise_var, targets, target_pos, layer_strength,
    layer_scale, tile_layer
):
    row_count, col_count = covariance.shape
    target_width = targets.shape[1]
    error_rows = target_width * n_col // n_row
    chunks = (target_width + col_count) // CHUNK

    def f32(*shape):
        return jax.ShapeDtypeStruct(shape, jnp.float32)

    vmem = pl.BlockSpec(memory_space=pltpu.VMEM)
    anywhere = pl.BlockSpec(memory_space=pltpu.HBM)
    smem = pl.BlockSpec(memory_space=pltpu.SMEM)
    dma = pltpu.SemaphoreType.DMA
    results = pl.pallas_call(
        functools.partial(panel_kernel, n_row, n_col),
        out_shape=(
            f32(row_count, col_count),
            f32(row_count, target_width),
            f32(row_count, PB),
            f32(error_rows, target_width),
        ),
        in_specs=[anywhere] * 4,
        out_specs=[vmem] * 4,
        scratch_shapes=[
            pltpu.VMEM((row_count, PB), jnp.float32),
            pltpu.VMEM((PB, target_width + col_count), jnp.float32),
            pltpu.VMEM((PB, error_rows), jnp.float32),
            pltpu.VMEM((3, HALF, HALF), jnp.float32),
            pltpu.VMEM((PB,), jnp.int32),
            pltpu.VMEM((row_count,), jnp.int32),
            pltpu.SMEM(noise_var.shape, jnp.float32),
            pltpu.VMEM((1, row_count), jnp.float32),
            pltpu.VMEM((HALF, PB), jnp.float32),
            pltpu.VMEM((PB, PB), jnp.float32),
            pltpu.VMEM((PB, PB), jnp.float32),
            pltpu.VMEM((row_count, 3 * PB), jnp.bfloat16),
            pltpu.VMEM((3 * PB, 2 * PB), jnp.bfloat16),
            dma((11,)),
            dma((col_count // PB,)),
            dma((4, 4)),
            dma((4,)),
            dma((chunks, 2)),
            dma((chunks,)),
            dma((ROW_CHUNKS, 2)),
            dma((ROW_CHUNKS, 2)),
            dma((n_col,)),
            dma,
        ],
        compiler_params=pltpu.CompilerParams(
            collective_id=0, has_side_effects=True, vmem_limit_bytes=16 * 1024 * 1024
        ),
        name="panel",
    )(
        covariance,
        *[pltpu.with_memory_space_constraint(x, pltpu.HBM) for x in (targets, wfs_map, noise_var)],
    )

    outs = pl.pallas_call(
        store_kernel,
        out_shape=(
            f32(row_count, col_count),
            f32(row_count, target_width),
            f32(row_count, PB),
            f32(error_rows, target_width),
        ),
        in_specs=[vmem] * 5 + [smem] * 3,
        out_specs=[anywhere] * 4,
        scratch_shapes=[pltpu.VMEM((error_rows, target_width), jnp.float32), dma((SLABS + 3,))],
        compiler_params=pltpu.CompilerParams(vmem_limit_bytes=4 * 1024 * 1024),
        name="store",
    )(*results, target_pos, layer_strength, layer_scale, tile_layer)
    updated, reconstructor, panel, error_cov = outs
    return updated, panel, reconstructor, error_cov


def solution(mesh):
    placed = (P("row", "col"), P("row"), P(), P("row", "col"), P(), P(), P(), P())
    return jax.shard_map(
        functools.partial(local, mesh.shape["row"], mesh.shape["col"]),
        mesh=mesh,
        in_specs=placed,
        out_specs=(P("row", "col"), P("row", None), P("row", "col"), P("row", "col")),
        check_vma=False,
    )
```

time: 121 us -> 78.3 us (0.65)
  the two profiles are of different devices: /device:TPU:31 before, /device:TPU:27 now
where the time goes in v1:
time: 78.3 us; the launch traced here: 78.2 us
  Pallas kernels  77.5 us (99%)
    pallas_call x1, Pallas kernels, local(): pl.pallas_call(functools.partial(panel_kernel, n_row, n_col), out_shape=(...  68.7 us
    pallas_call x1, Pallas kernels, local(): pl.pallas_call(store_kernel, out_shape=(f32(row_count, col_count), f32(ro...  8.72 us

profile of v1, /device:TPU:27, one launch (start us, length us, event | category | flops | bytes accessed | tf_op | source)
XLA Modules:
  0.0 78.2 jit_solution(9464013177009696342)
XLA Ops:
  0.6 0.0 copy-start.3
  0.6 0.0 copy-start.2
  0.7 0.0 copy-start.1
  0.7 0.0 copy-start
  0.7 68.7 %panel.1 = (f32[1536,3072]{1,0:T(8,128)S(1)}, f32[1536,512]{1,0:T(8,128)S(1)}, f32[1536,256]{1,0:T(8,128)S(1)}, f32[256,512]{1,0:T(8,128)S(1)}) custom-call(f32[1536,3072]{1,0:T(8,128)} %cov.1, f32[1536,512]{1,0:T(8,128)} %targets.1, s32[1536]{0:T(1024)} %sensors.1, f32[6]{0:T(128)} %noise_var.1), custom_call_target="tpu_custom_call" | custom-call | tf_op jit(solution)/shard_map/panel/pallas_call | solution.py:627
  69.4 0.0 copy-done.3
  69.4 0.0 copy-done.2
  69.4 0.0 copy-done.1
  69.4 0.0 copy-done
  69.5 8.7 %store.1 = (f32[1536,3072]{1,0:T(8,128)}, f32[1536,512]{1,0:T(8,128)}, f32[1536,256]{1,0:T(8,128)}, f32[256,512]{1,0:T(8,128)}) custom-call(f32[1536,3072]{1,0:T(8,128)S(1)} %get-tuple-element.12.updated, f32[1536,512]{1,0:T(8,128)S(1)} %get-tuple-element.13.reconstructor, f32[1536,256]{1,0:T(8,128)S(1)} %get-tuple-element.14.panel, ...), custom_call_target="tpu_custom_call" | custom-call | tf_op jit(solution)/shard_map/store/pallas_call | solution.py:671
Async XLA Ops:
  0.6 68.8 %copy-start.3 = (s32[16]{0:T(128)S(1)}, s32[16]{0:T(128)}, u32[]{:S(2)}) copy-start(s32[16]{0:T(128)} %tile_layer.1) | copy-start | bytes 196
  0.6 68.8 %copy-start.2 = (f32[35]{0:T(128)S(1)}, f32[35]{0:T(128)}, u32[]{:S(2)}) copy-start(f32[35]{0:T(128)} %scale.1) | copy-start | bytes 424
  0.7 68.8 %copy-start.1 = (f32[35]{0:T(128)S(1)}, f32[35]{0:T(128)}, u32[]{:S(2)}) copy-start(f32[35]{0:T(128)} %strength.1) | copy-start | bytes 424
  0.7 68.8 %copy-start = (f32[2,2048]{1,0:T(2,128)S(1)}, f32[2,2048]{1,0:T(2,128)}, u32[]{:S(2)}) copy-start(f32[2,2048]{1,0:T(2,128)} %pos.1) | copy-start | bytes 49156

commit v2 on v1

--- a/solution.py
+++ b/solution.py
@@ -12,9 +12,10 @@
 HALF = PB // 2
 STEP = 8
 CHUNK = 128
+GROUP = 4
 ROW_CHUNKS = 12
-AHEAD = 2
-LATE = 2
+AHEAD = 3
+LATE = 3
 
 MESH = pl.DeviceIdType.MESH
 precise = lax.Precision.HIGHEST
@@ -55,6 +56,7 @@
 
 def target_covariance(out, product, pos, strength, scale, tile_layer, row_start, col_start):
     height, width = out.shape
+    levels = strength.shape[0]
 
     def upright(axis):
         line = pos[pl.ds(axis, 1), pl.ds(row_start, height)]
@@ -71,10 +73,21 @@
                 tile_layer[row_start // TILE + i], tile_layer[col_start // TILE + j]
             )
 
-            def layer(l, total, distance=distance):
-                return total + strength[l] / (1.0 + distance * (1.0 / (scale[l] * scale[l])))
-
-            total = lax.fori_loop(0, lowest + 1, layer, jnp.zeros_like(distance))
+            def layers(g, total, distance=distance, lowest=lowest):
+                terms = []
+                for k in range(GROUP):
+                    l = jnp.minimum(g * GROUP + k, levels - 1)
+                    weight = jnp.where(g * GROUP + k <= lowest, strength[l], 0.0)
+                    square = scale[l] * scale[l]
+                    terms.append((weight * square, square + distance))
+                while len(terms) > 1:
+                    terms = [
+                        (a[0] * b[1] + b[0] * a[1], a[1] * b[1])
+                        for a, b in zip(terms[::2], terms[1::2])
+                    ]
+                return total + terms[0][0] / terms[0][1]
+
+            total = lax.fori_loop(0, lax.div(lowest, GROUP) + 1, layers, jnp.zeros_like(distance))
             here = (pl.ds(i * TILE, TILE), pl.ds(j * TILE, TILE))
             out[here] = total - product[here]
 
@@ -148,6 +161,7 @@
     inverse_ref,
     parts,
     solver,
+    head_ref,
     local_sem,
     cov_sem,
     diag_send,
@@ -177,6 +191,7 @@
     relays = even & (r > 0)
     first = (r == 0) & (c == 0)
     half_ring = n_col // 2
+    ahead = jnp.where(place == half_ring, AHEAD + 2, AHEAD)
 
     head_span = pl.ds(0, width)
     head_copy = pltpu.make_async_copy(
@@ -339,18 +354,21 @@
         return total
 
     def row_goal(s):
-        late = jnp.where(place == half_ring, 7, 2) + jnp.where(plane == 0, 3, 0)
-        return jnp.clip(lax.div(jnp.maximum(s + 4 * plane - late, 0), 3), 0, ROW_CHUNKS)
+        late = jnp.where(place == half_ring, 1, 0) + jnp.where(plane == 0, 3, -1)
+        reach = lax.div(jnp.maximum(s + lax.div(14 * plane, 3) - late, 0), 3)
+        return jnp.minimum(reach, ROW_CHUNKS)
 
     for i in range(4):
         diag_each(i, True, first, start)
-    run((r == 0) & (c > 0), lambda: each(0, AHEAD, source_chunk))
-    run((place == 0) & ((r == 0) | (r > 1)), lambda: each(0, ROW_CHUNKS, row_source))
+    run((r == 0) & (c > 0), lambda: each(0, ahead, source_chunk))
+    run((place == 0) & (r != 1), lambda: each(0, ROW_CHUNKS, row_source))
     run(first, lambda: each(0, chunks, source_chunk))
-    run(c > 0, lambda: takes(0, AHEAD))
-    each(0, row_goal(-1), row_forward)
+    run(c > 0, lambda: takes(0, ahead))
+    early_rows = jnp.maximum(row_goal(-1) - 1, 0)
+    each(0, early_rows, row_forward)
     diag_pass(0)
     diag_pass(1)
+    run((place == 0) & (r == 1), lambda: each(0, ROW_CHUNKS, row_source))
     sensor_copy.wait()
     noise_copy.wait()
     noise[...] = noise_of(own_sensors[...].reshape(1, row_count))
@@ -360,8 +378,8 @@
     )
 
     def chunk_goal(s):
-        late = jnp.where(c == 0, 5, 1)
-        return jnp.maximum(lax.div(jnp.maximum(s - late, 0), 3), jnp.where(c == 0, 0, AHEAD))
+        early = jnp.where(has_far, jnp.where(c == 0, -1, 7), -3)
+        return jnp.maximum(lax.div(jnp.maximum(s + early, 0), 3), jnp.where(c == 0, 0, ahead))
 
     steps = HALF // STEP
 
@@ -373,8 +391,7 @@
         @pl.when(s == 4)
         def _():
             diag_pass(3)
-            run((place == 0) & (r == 1), lambda: each(0, ROW_CHUNKS, row_source))
-            run((r == 0) & (c > 0), lambda: each(AHEAD, chunks, source_chunk))
+            run((r == 0) & (c > 0), lambda: each(ahead, chunks, source_chunk))
 
         @pl.when(s == 6)
         def _():
@@ -384,7 +401,7 @@
         run(s == 8, target_copy.start)
         run((lax.rem(s, 2) == 1) & (lax.div(s, 2) < pairs), lambda: cov_copy(lax.div(s, 2)).start())
         takes(chunk_goal(s - 1), chunk_goal(s))
-        each(row_goal(s - 1), row_goal(s), row_forward)
+        each(jnp.where(s > 0, row_goal(s - 1), early_rows), row_goal(s), row_forward)
 
     def half(block, where):
         t_ref[:, pl.ds(0, HALF)] = block
@@ -408,8 +425,6 @@
     )
 
     def need_start():
-        run(r == 0, head_copy.wait)
-        run(~even, lambda: each(0, head_chunks, chunk_take))
         for k in range(n_col):
             run((c == owner) & (c != k), need_copies[k].start)
         run(c == owner, own_need.start)
@@ -436,25 +451,36 @@
         inverse_22, dot(lower, inverse_ref[pl.ds(0, HALF), pl.ds(0, HALF)])
     )
     last = 2 * steps - 1
-    each(row_goal(last), ROW_CHUNKS, row_forward)
     goal = chunk_goal(last)
-    takes(goal, goal + LATE)
-    goal = goal + LATE
+
+    def keep_up(goal, more, wanted=True):
+        more = jnp.where(has_far & wanted, more, 0)
+        takes(goal, goal + more)
+        return goal + more
+
 
     inverse = inverse_ref[...]
     solver[:, pl.ds(0, PB)] = stacked(inverse.T)
     solver[:, pl.ds(PB, PB)] = stacked(dot(inverse, inverse, ((0,), (0,))))
 
+    goal = keep_up(goal, 3)
+    each(row_goal(last), ROW_CHUNKS, row_forward)
+    run(r == 0, head_copy.wait)
+    run(~even, lambda: each(0, head_chunks, chunk_take))
+    head_ref[...] = dot(inverse, col_raw[:, head_span])
+    goal = keep_up(goal, 1)
+
     def row_wait(j):
         for way in range(2):
             run((place > 0) & ~forwards(way), row_copies(j, way, False).wait_recv)
 
-    each(0, ROW_CHUNKS, row_wait)
+    each(0, ROW_CHUNKS - LATE, row_wait)
+    for j in range(LATE):
+        goal = keep_up(goal, 1, c > 0)
+        row_wait(ROW_CHUNKS - LATE + j)
     run(c == 0, row_copy.wait)
-    takes(goal, goal + 1)
-    goal = goal + 1
     need_start()
-    each(min(2 * steps // 2, pairs), pairs, lambda p: cov_copy(p).start())
+    each(min(steps, pairs), pairs, lambda p: cov_copy(p).start())
 
     def solve(i, carry):
         rows = pl.ds(pl.multiple_of(i * PB, PB), PB)
@@ -477,10 +503,7 @@
     def _():
         panel[pl.ds(0, PB), :] = factor_ref[...]
 
-    takes(goal, goal + 1)
-    goal = goal + 1
-
-    head = dot(inverse, col_raw[:, head_span])
+    goal = keep_up(goal, 1)
     target_copy.wait()
     reconstructor[...] = reconstructor[...] - jnp.dot(
         parts[...], stacked(col_raw[:, head_span]), preferred_element_type=jnp.float32
@@ -488,8 +511,9 @@
 
     @pl.when(r == 0)
     def _():
-        reconstructor[pl.ds(0, PB), :] = head
-
+        reconstructor[pl.ds(0, PB), :] = head_ref[...]
+
+    goal = keep_up(goal, 1)
     run(r == 0, col_copy.wait)
 
     def reach(p):
@@ -526,7 +550,7 @@
     def finish_product():
         run(c == owner, own_need.wait)
         run(c != owner, need_copies[0].wait_recv)
-        product[...] = dot(dot(inverse, need_raw[...]), head, ((0,), (0,)))
+        product[...] = dot(dot(inverse, need_raw[...]), head_ref[...], ((0,), (0,)))
 
     tail = pairs - pairs // 6
     each(0, tail, update)
@@ -648,6 +672,7 @@
             pltpu.VMEM((PB, PB), jnp.float32),
             pltpu.VMEM((row_count, 3 * PB), jnp.bfloat16),
             pltpu.VMEM((3 * PB, 2 * PB), jnp.bfloat16),
+            pltpu.VMEM((PB, target_width), jnp.float32),
             dma((11,)),
             dma((col_count // PB,)),
             dma((4, 4)),

time: 78.3 us -> 71.7 us (0.916)
  the two profiles are of different devices: /device:TPU:27 before, /device:TPU:31 now
where the time goes in v2:
time: 71.7 us; the launch traced here: 71.6 us
  Pallas kernels  70.8 us (99%)
    pallas_call x1, Pallas kernels, local(): pl.pallas_call(functools.partial(panel_kernel, n_row, n_col), out_shape=(...  62.1 us
    pallas_call x1, Pallas kernels, local(): pl.pallas_call(store_kernel, out_shape=(f32(row_count, col_count), f32(ro...  8.72 us

profile of v2, /device:TPU:31, one launch (start us, length us, event | category | flops | bytes accessed | tf_op | source)
XLA Modules:
  0.0 71.6 jit_solution(10101519385934649113)
XLA Ops:
  0.6 0.0 copy-start.3
  0.6 0.0 copy-start.2
  0.7 0.0 copy-start.1
  0.7 0.0 copy-start
  0.7 62.1 %panel.1 = (f32[1536,3072]{1,0:T(8,128)S(1)}, f32[1536,512]{1,0:T(8,128)S(1)}, f32[1536,256]{1,0:T(8,128)S(1)}, f32[256,512]{1,0:T(8,128)S(1)}) custom-call(f32[1536,3072]{1,0:T(8,128)} %cov.1, f32[1536,512]{1,0:T(8,128)} %targets.1, s32[1536]{0:T(1024)} %sensors.1, f32[6]{0:T(128)} %noise_var.1), custom_call_target="tpu_custom_call" | custom-call | tf_op jit(solution)/shard_map/panel/pallas_call | solution.py:651
  62.8 0.0 copy-done.3
  62.8 0.0 copy-done.2
  62.8 0.0 copy-done.1
  62.8 0.0 copy-done
  62.9 8.7 %store.1 = (f32[1536,3072]{1,0:T(8,128)}, f32[1536,512]{1,0:T(8,128)}, f32[1536,256]{1,0:T(8,128)}, f32[256,512]{1,0:T(8,128)}) custom-call(f32[1536,3072]{1,0:T(8,128)S(1)} %get-tuple-element.12.updated, f32[1536,512]{1,0:T(8,128)S(1)} %get-tuple-element.13.reconstructor, f32[1536,256]{1,0:T(8,128)S(1)} %get-tuple-element.14.panel, ...), custom_call_target="tpu_custom_call" | custom-call | tf_op jit(solution)/shard_map/store/pallas_call | solution.py:696
Async XLA Ops:
  0.6 62.2 %copy-start.3 = (s32[16]{0:T(128)S(1)}, s32[16]{0:T(128)}, u32[]{:S(2)}) copy-start(s32[16]{0:T(128)} %tile_layer.1) | copy-start | bytes 196
  0.6 62.2 %copy-start.2 = (f32[35]{0:T(128)S(1)}, f32[35]{0:T(128)}, u32[]{:S(2)}) copy-start(f32[35]{0:T(128)} %scale.1) | copy-start | bytes 424
  0.7 62.2 %copy-start.1 = (f32[35]{0:T(128)S(1)}, f32[35]{0:T(128)}, u32[]{:S(2)}) copy-start(f32[35]{0:T(128)} %strength.1) | copy-start | bytes 424
  0.7 62.2 %copy-start = (f32[2,2048]{1,0:T(2,128)S(1)}, f32[2,2048]{1,0:T(2,128)}, u32[]{:S(2)}) copy-start(f32[2,2048]{1,0:T(2,128)} %pos.1) | copy-start | bytes 49156

commit v3 on v2

--- a/solution.py
+++ b/solution.py
@@ -12,6 +12,7 @@
 HALF = PB // 2
 STEP = 8
 CHUNK = 128
+SPLIT = 1
 GROUP = 4
 ROW_CHUNKS = 12
 AHEAD = 3
@@ -179,8 +180,8 @@
     width = reconstructor.shape[1]
     need = need_raw.shape[1]
     pairs = col_count // PB
-    head_chunks = width // CHUNK
-    chunks = head_chunks + col_count // CHUNK
+    head_chunks = SPLIT * width // CHUNK
+    chunks = head_chunks + SPLIT * col_count // CHUNK
     even = lax.rem(r, 2) == 0
     plane = lax.div(r, 2)
     place, after, before = gray_neighbours(c, n_col)
@@ -191,7 +192,7 @@
     relays = even & (r > 0)
     first = (r == 0) & (c == 0)
     half_ring = n_col // 2
-    ahead = jnp.where(place == half_ring, AHEAD + 2, AHEAD)
+    ahead = SPLIT * jnp.where(place == half_ring, AHEAD + 2, AHEAD)
 
     head_span = pl.ds(0, width)
     head_copy = pltpu.make_async_copy(
@@ -280,12 +281,16 @@
     def finish(copy):
         copy.wait_send()
 
+    piece_rows = PB // SPLIT
+
     def span(q):
-        return pl.ds(pl.multiple_of(q * CHUNK, CHUNK), CHUNK)
+        rows = pl.ds(pl.multiple_of(lax.rem(q, SPLIT) * piece_rows, piece_rows), piece_rows)
+        columns = pl.ds(pl.multiple_of(lax.div(q, SPLIT) * CHUNK, CHUNK), CHUNK)
+        return rows, columns
 
     def chunk_copies(q, src):
         return upward(
-            src, col_raw.at[:, span(q)], [col_send.at[q, 0], col_send.at[q, 1]], col_recv.at[q]
+            src, col_raw.at[span(q)], [col_send.at[q, 0], col_send.at[q, 1]], col_recv.at[q]
         )
 
     def chunk_start(copies):
@@ -296,13 +301,13 @@
         run(
             q < head_chunks,
             lambda: chunk_start(
-                chunk_copies(q, targets.at[pl.ds(0, PB), span(jnp.minimum(q, head_chunks - 1))])
+                chunk_copies(q, targets.at[span(jnp.minimum(q, head_chunks - 1))])
             ),
         )
         run(
             q >= head_chunks,
             lambda: chunk_start(
-                chunk_copies(q, cov.at[pl.ds(0, PB), span(jnp.maximum(q - head_chunks, 0))])
+                chunk_copies(q, cov.at[span(jnp.maximum(q - head_chunks, 0))])
             ),
         )
 
@@ -314,7 +319,7 @@
         lax.fori_loop(low, high, body, 0)
 
     def chunk_take(q):
-        copies = chunk_copies(q, col_raw.at[:, span(q)])
+        copies = chunk_copies(q, col_raw.at[span(q)])
         copies[0].wait_recv()
         run(even, lambda: chunk_start(copies))
 
@@ -378,8 +383,10 @@
     )
 
     def chunk_goal(s):
-        early = jnp.where(has_far, jnp.where(c == 0, -1, 7), -3)
-        return jnp.maximum(lax.div(jnp.maximum(s + early, 0), 3), jnp.where(c == 0, 0, ahead))
+        early = jnp.where(c == 0, -1, jnp.where(place == half_ring, 12, 7))
+        early = jnp.where(has_far, early, -3)
+        reached = lax.div(SPLIT * jnp.maximum(s + early, 0), 3)
+        return jnp.maximum(reached, jnp.where(c == 0, 0, ahead))
 
     steps = HALF // STEP
 
@@ -454,7 +461,7 @@
     goal = chunk_goal(last)
 
     def keep_up(goal, more, wanted=True):
-        more = jnp.where(has_far & wanted, more, 0)
+        more = jnp.where(has_far & wanted, SPLIT * more, 0)
         takes(goal, goal + more)
         return goal + more
 
@@ -476,7 +483,7 @@
 
     each(0, ROW_CHUNKS - LATE, row_wait)
     for j in range(LATE):
-        goal = keep_up(goal, 1, c > 0)
+        goal = keep_up(goal, 1, (c > 0) & (place != half_ring))
         row_wait(ROW_CHUNKS - LATE + j)
     run(c == 0, row_copy.wait)
     need_start()
@@ -517,13 +524,15 @@
     run(r == 0, col_copy.wait)
 
     def reach(p):
-        return jnp.minimum(jnp.maximum(goal + p, head_chunks + 2 * p), chunks)
+        return jnp.minimum(jnp.maximum(goal + SPLIT * p, head_chunks + 2 * SPLIT * p), chunks)
 
     def update(p):
         takes(reach(p), reach(p + 1))
         run(
             ~even,
-            lambda: each(head_chunks + 2 * p, head_chunks + 2 * p + 2, chunk_take),
+            lambda: each(
+                head_chunks + 2 * SPLIT * p, head_chunks + 2 * SPLIT * (p + 1), chunk_take
+            ),
         )
         cov_copy(p).wait()
         columns = pl.ds(pl.multiple_of(p * PB, PB), PB)
@@ -555,11 +564,12 @@
     tail = pairs - pairs // 6
     each(0, tail, update)
     finish_product()
-    each(tail, pairs, update)
 
     @pl.when(c == 0)
     def _():
         updated[:, pl.ds(0, PB)] = panel[...]
+
+    each(tail, pairs, update)
 
     for k in range(n_col):
         run((c == owner) & (c != k), need_copies[k].wait_send)
@@ -567,7 +577,7 @@
         diag_each(i, False, r >= 0, finish)
 
     def chunk_finish(q):
-        copies = chunk_copies(q, col_raw.at[:, span(q)])
+        copies = chunk_copies(q, col_raw.at[span(q)])
         run(has_far, copies[0].wait_send)
         run(has_near, copies[1].wait_send)
 
@@ -639,7 +649,7 @@
     row_count, col_count = covariance.shape
     target_width = targets.shape[1]
     error_rows = target_width * n_col // n_row
-    chunks = (target_width + col_count) // CHUNK
+    chunks = SPLIT * (target_width + col_count) // CHUNK
 
     def f32(*shape):
         return jax.ShapeDtypeStruct(shape, jnp.float32)

time: 71.7 us -> 69.1 us (0.964)
  Pallas kernels: 70.8 us -> 68.2 us
    pallas_call x1, Pallas kernels: 62.1 us -> 59.5 us  [local(): pl.pallas_call(functools.partial(panel_kernel, n_row, n_col), out_shape=(...]
where the time goes in v3:
time: 69.1 us; the launch traced here: 69 us
  Pallas kernels  68.2 us (99%)
  between operations  0.7 us (1%)
    pallas_call x1, Pallas kernels, local(): pl.pallas_call(functools.partial(panel_kernel, n_row, n_col), out_shape=(...  59.5 us
    pallas_call x1, Pallas kernels, local(): pl.pallas_call(store_kernel, out_shape=(f32(row_count, col_count), f32(ro...  8.72 us

profile of v3, /device:TPU:31, one launch (start us, length us, event | category | flops | bytes accessed | tf_op | source)
XLA Modules:
  0.0 69.0 jit_solution(11842351514303508087)
XLA Ops:
  0.6 0.0 copy-start.3
  0.6 0.0 copy-start.2
  0.7 0.0 copy-start.1
  0.7 0.0 copy-start
  0.7 59.5 %panel.1 = (f32[1536,3072]{1,0:T(8,128)S(1)}, f32[1536,512]{1,0:T(8,128)S(1)}, f32[1536,256]{1,0:T(8,128)S(1)}, f32[256,512]{1,0:T(8,128)S(1)}) custom-call(f32[1536,3072]{1,0:T(8,128)} %cov.1, f32[1536,512]{1,0:T(8,128)} %targets.1, s32[1536]{0:T(1024)} %sensors.1, f32[6]{0:T(128)} %noise_var.1), custom_call_target="tpu_custom_call" | custom-call | tf_op jit(solution)/shard_map/panel/pallas_call | solution.py:661
  60.2 0.0 copy-done.3
  60.2 0.0 copy-done.2
  60.2 0.0 copy-done.1
  60.2 0.0 copy-done
  60.2 8.7 %store.1 = (f32[1536,3072]{1,0:T(8,128)}, f32[1536,512]{1,0:T(8,128)}, f32[1536,256]{1,0:T(8,128)}, f32[256,512]{1,0:T(8,128)}) custom-call(f32[1536,3072]{1,0:T(8,128)S(1)} %get-tuple-element.12.updated, f32[1536,512]{1,0:T(8,128)S(1)} %get-tuple-element.13.reconstructor, f32[1536,256]{1,0:T(8,128)S(1)} %get-tuple-element.14.panel, ...), custom_call_target="tpu_custom_call" | custom-call | tf_op jit(solution)/shard_map/store/pallas_call | solution.py:706
Async XLA Ops:
  0.6 59.6 %copy-start.3 = (s32[16]{0:T(128)S(1)}, s32[16]{0:T(128)}, u32[]{:S(2)}) copy-start(s32[16]{0:T(128)} %tile_layer.1) | copy-start | bytes 196
  0.6 59.6 %copy-start.2 = (f32[35]{0:T(128)S(1)}, f32[35]{0:T(128)}, u32[]{:S(2)}) copy-start(f32[35]{0:T(128)} %scale.1) | copy-start | bytes 424
  0.7 59.6 %copy-start.1 = (f32[35]{0:T(128)S(1)}, f32[35]{0:T(128)}, u32[]{:S(2)}) copy-start(f32[35]{0:T(128)} %strength.1) | copy-start | bytes 424
  0.7 59.6 %copy-start = (f32[2,2048]{1,0:T(2,128)S(1)}, f32[2,2048]{1,0:T(2,128)}, u32[]{:S(2)}) copy-start(f32[2,2048]{1,0:T(2,128)} %pos.1) | copy-start | bytes 49156

commit v4 on v3

--- a/solution.py
+++ b/solution.py
@@ -12,7 +12,11 @@
 HALF = PB // 2
 STEP = 8
 CHUNK = 128
-SPLIT = 1
+TAIL = 4
+KEEP = 3
+MEET = 1
+PUSH = (3, 3)
+PACE = (9, 9)
 GROUP = 4
 ROW_CHUNKS = 12
 AHEAD = 3
@@ -138,6 +142,27 @@
         action()
 
 
+def update_pair(out, out_columns, matrix, columns, parts, raw, noise, begin, r):
+    height = parts.shape[0]
+    out[:, out_columns] = matrix[:, columns] - jnp.dot(
+        parts[...], stacked(raw), preferred_element_type=jnp.float32
+    )
+
+    @pl.when((begin >= 0) & (begin < height))
+    def _():
+        block = pl.ds(pl.multiple_of(begin, PB), PB)
+        diagonal = lax.broadcasted_iota(jnp.int32, (PB, PB), 0) == (
+            lax.broadcasted_iota(jnp.int32, (PB, PB), 1)
+        )
+        out[block, out_columns] = out[block, out_columns] + jnp.where(
+            diagonal, noise[:, block], 0.0
+        )
+
+    @pl.when(r == 0)
+    def _():
+        out[pl.ds(0, PB), out_columns] = jnp.zeros((PB, PB), jnp.float32)
+
+
 def panel_kernel(
     n_row,
     n_col,
@@ -149,6 +174,9 @@
     reconstructor,
     panel,
     product,
+    parts,
+    noise,
+    late_raw,
     row_raw,
     col_raw,
     need_raw,
@@ -156,11 +184,9 @@
     head_sensors,
     own_sensors,
     kinds,
-    noise,
     t_ref,
     factor_ref,
     inverse_ref,
-    parts,
     solver,
     head_ref,
     local_sem,
@@ -169,6 +195,8 @@
     diag_recv,
     col_send,
     col_recv,
+    tail_send,
+    tail_recv,
     row_send,
     row_recv,
     need_send,
@@ -180,8 +208,8 @@
     width = reconstructor.shape[1]
     need = need_raw.shape[1]
     pairs = col_count // PB
-    head_chunks = SPLIT * width // CHUNK
-    chunks = head_chunks + SPLIT * col_count // CHUNK
+    head_chunks = width // CHUNK
+    chunks = head_chunks + (col_count - PB) // CHUNK
     even = lax.rem(r, 2) == 0
     plane = lax.div(r, 2)
     place, after, before = gray_neighbours(c, n_col)
@@ -192,7 +220,7 @@
     relays = even & (r > 0)
     first = (r == 0) & (c == 0)
     half_ring = n_col // 2
-    ahead = SPLIT * jnp.where(place == half_ring, AHEAD + 2, AHEAD)
+    ahead = jnp.where(place == half_ring, AHEAD + 2, AHEAD)
 
     head_span = pl.ds(0, width)
     head_copy = pltpu.make_async_copy(
@@ -281,12 +309,10 @@
     def finish(copy):
         copy.wait_send()
 
-    piece_rows = PB // SPLIT
+    tail_rows = PB // TAIL
 
     def span(q):
-        rows = pl.ds(pl.multiple_of(lax.rem(q, SPLIT) * piece_rows, piece_rows), piece_rows)
-        columns = pl.ds(pl.multiple_of(lax.div(q, SPLIT) * CHUNK, CHUNK), CHUNK)
-        return rows, columns
+        return pl.ds(0, PB), pl.ds(pl.multiple_of(q * CHUNK, CHUNK), CHUNK)
 
     def chunk_copies(q, src):
         return upward(
@@ -311,6 +337,20 @@
             ),
         )
 
+    def tail_copies(t, source):
+        rows = pl.ds(pl.multiple_of(t * tail_rows, tail_rows), tail_rows)
+        dst = col_raw.at[rows, pl.ds(width + col_count - PB, PB)]
+        src = cov.at[rows, pl.ds(col_count - PB, PB)] if source else dst
+        return upward(src, dst, [tail_send.at[t, 0], tail_send.at[t, 1]], tail_recv.at[t])
+
+    def tail_take(t):
+        copies = tail_copies(t, False)
+        copies[0].wait_recv()
+        run(even, lambda: chunk_start(copies))
+
+    def tail_source(t):
+        chunk_start(tail_copies(t, True))
+
     def each(low, high, action):
         def body(i, carry):
             action(i)
@@ -367,7 +407,7 @@
         diag_each(i, True, first, start)
     run((r == 0) & (c > 0), lambda: each(0, ahead, source_chunk))
     run((place == 0) & (r != 1), lambda: each(0, ROW_CHUNKS, row_source))
-    run(first, lambda: each(0, chunks, source_chunk))
+    run(first, lambda: (each(0, chunks, source_chunk), each(0, TAIL, tail_source)))
     run(c > 0, lambda: takes(0, ahead))
     early_rows = jnp.maximum(row_goal(-1) - 1, 0)
     each(0, early_rows, row_forward)
@@ -385,7 +425,7 @@
     def chunk_goal(s):
         early = jnp.where(c == 0, -1, jnp.where(place == half_ring, 12, 7))
         early = jnp.where(has_far, early, -3)
-        reached = lax.div(SPLIT * jnp.maximum(s + early, 0), 3)
+        reached = lax.div(jnp.maximum(s + early, 0), 3)
         return jnp.maximum(reached, jnp.where(c == 0, 0, ahead))
 
     steps = HALF // STEP
@@ -398,7 +438,10 @@
         @pl.when(s == 4)
         def _():
             diag_pass(3)
-            run((r == 0) & (c > 0), lambda: each(ahead, chunks, source_chunk))
+            run(
+                (r == 0) & (c > 0),
+                lambda: (each(ahead, chunks, source_chunk), each(0, TAIL, tail_source)),
+            )
 
         @pl.when(s == 6)
         def _():
@@ -461,7 +504,7 @@
     goal = chunk_goal(last)
 
     def keep_up(goal, more, wanted=True):
-        more = jnp.where(has_far & wanted, SPLIT * more, 0)
+        more = jnp.where(has_far & wanted, more, 0)
         takes(goal, goal + more)
         return goal + more
 
@@ -470,7 +513,7 @@
     solver[:, pl.ds(0, PB)] = stacked(inverse.T)
     solver[:, pl.ds(PB, PB)] = stacked(dot(inverse, inverse, ((0,), (0,))))
 
-    goal = keep_up(goal, 3)
+    goal = keep_up(goal, jnp.where(plane == 1, PUSH[0], PUSH[1]))
     each(row_goal(last), ROW_CHUNKS, row_forward)
     run(r == 0, head_copy.wait)
     run(~even, lambda: each(0, head_chunks, chunk_take))
@@ -523,71 +566,87 @@
     goal = keep_up(goal, 1)
     run(r == 0, col_copy.wait)
 
+    pace = jnp.where(plane == 1, PACE[0], PACE[1])
+
     def reach(p):
-        return jnp.minimum(jnp.maximum(goal + SPLIT * p, head_chunks + 2 * SPLIT * p), chunks)
-
-    def update(p):
+        return jnp.minimum(jnp.maximum(goal + lax.div(pace * p, 9), head_chunks + 2 * p), chunks)
+
+    def tail_reach(p):
+        reached = jnp.clip(TAIL * (goal + lax.div(pace * p, 9) - chunks) // 2, 0, TAIL)
+        return jnp.where(p == pairs, TAIL, reached)
+
+    def arrive(p):
         takes(reach(p), reach(p + 1))
         run(
-            ~even,
-            lambda: each(
-                head_chunks + 2 * SPLIT * p, head_chunks + 2 * SPLIT * (p + 1), chunk_take
-            ),
-        )
+            ~even & (p < pairs - 1),
+            lambda: each(head_chunks + 2 * p, head_chunks + 2 * p + 2, chunk_take),
+        )
+        run(relays, lambda: each(tail_reach(p), tail_reach(p + 1), tail_take))
+        run(~even & (p == pairs - 1), lambda: each(0, TAIL, tail_take))
         cov_copy(p).wait()
+
+    def update(p):
+        arrive(p)
         columns = pl.ds(pl.multiple_of(p * PB, PB), PB)
-        raw = col_raw[:, pl.ds(pl.multiple_of(width + p * PB, CHUNK), PB)]
-        updated[:, columns] = updated[:, columns] - jnp.dot(
-            parts[...], stacked(raw), preferred_element_type=jnp.float32
-        )
-        begin = c * col_count + p * PB - r * row_count
-
-        @pl.when((begin >= 0) & (begin < row_count))
-        def _():
-            block = pl.ds(pl.multiple_of(begin, PB), PB)
-            diagonal = lax.broadcasted_iota(jnp.int32, (PB, PB), 0) == (
-                lax.broadcasted_iota(jnp.int32, (PB, PB), 1)
-            )
-            updated[block, columns] = updated[block, columns] + jnp.where(
-                diagonal, noise[:, block], 0.0
-            )
-
-        @pl.when(r == 0)
-        def _():
-            updated[pl.ds(0, PB), columns] = jnp.zeros((PB, PB), jnp.float32)
+        update_pair(
+            updated,
+            columns,
+            updated,
+            columns,
+            parts,
+            col_raw[:, pl.ds(pl.multiple_of(width + p * PB, CHUNK), PB)],
+            noise,
+            c * col_count + p * PB - r * row_count,
+            r,
+        )
 
     def finish_product():
         run(c == owner, own_need.wait)
         run(c != owner, need_copies[0].wait_recv)
         product[...] = dot(dot(inverse, need_raw[...]), head_ref[...], ((0,), (0,)))
 
-    tail = pairs - pairs // 6
-    each(0, tail, update)
-    finish_product()
-
-    @pl.when(c == 0)
-    def _():
-        updated[:, pl.ds(0, PB)] = panel[...]
-
-    each(tail, pairs, update)
-
-    for k in range(n_col):
-        run((c == owner) & (c != k), need_copies[k].wait_send)
-    for i in range(4):
-        diag_each(i, False, r >= 0, finish)
-
     def chunk_finish(q):
         copies = chunk_copies(q, col_raw.at[span(q)])
         run(has_far, copies[0].wait_send)
         run(has_near, copies[1].wait_send)
 
-    each(0, chunks, chunk_finish)
-
     def row_finish(j):
         for way in range(2):
             run((place == 0) | forwards(way), row_copies(j, way, False).wait_send)
 
-    each(0, ROW_CHUNKS, row_finish)
+    tail = pairs - MEET
+    here = pairs - KEEP
+    settled = jnp.where(even, jnp.minimum(head_chunks + 2 * tail, chunks) - 4, 0)
+
+    def settle():
+        for k in range(n_col):
+            run((c == owner) & (c != k), need_copies[k].wait_send)
+        for i in range(4):
+            diag_each(i, False, r >= 0, finish)
+        run(even, lambda: each(0, settled, chunk_finish))
+        each(0, ROW_CHUNKS, row_finish)
+
+    each(0, min(tail, here), update)
+    each(min(tail, here), tail, arrive)
+    finish_product()
+    settle()
+
+    @pl.when(c == 0)
+    def _():
+        updated[:, pl.ds(0, PB)] = panel[...]
+
+    each(tail, max(tail, here), update)
+    each(max(tail, here), pairs, arrive)
+    late_raw[...] = col_raw[:, pl.ds(width + col_count - KEEP * PB, KEEP * PB)]
+
+    run(even, lambda: each(settled, chunks, chunk_finish))
+
+    def tail_finish(t):
+        copies = tail_copies(t, False)
+        run(has_far, copies[0].wait_send)
+        run(has_near, copies[1].wait_send)
+
+    each(0, TAIL, tail_finish)
 
 
 SLABS = 6
@@ -598,6 +657,9 @@
     reconstructor,
     panel,
     product,
+    parts,
+    noise,
+    late_raw,
     pos,
     strength,
     scale,
@@ -607,15 +669,18 @@
     panel_out,
     error_out,
     error,
+    late,
     sems,
 ):
     r = lax.axis_index("row")
     c = lax.axis_index("col")
-    slab = updated.shape[0] // SLABS
+    row_count, col_count = updated.shape
+    slab = row_count // SLABS
+    early = pl.ds(0, col_count - KEEP * PB)
     copies = [
         pltpu.make_async_copy(
-            updated.at[pl.ds(i * slab, slab), :],
-            updated_out.at[pl.ds(i * slab, slab), :],
+            updated.at[pl.ds(i * slab, slab), early],
+            updated_out.at[pl.ds(i * slab, slab), early],
             sems.at[i],
         )
         for i in range(SLABS)
@@ -624,6 +689,32 @@
     copies.append(pltpu.make_async_copy(panel, panel_out, sems.at[SLABS + 1]))
     for copy in copies:
         copy.start()
+
+    def late_copy(k):
+        columns = pl.ds(pl.multiple_of(k * PB, PB), PB)
+        place = pl.ds(pl.multiple_of(col_count - (KEEP - k) * PB, PB), PB)
+        return pltpu.make_async_copy(
+            late.at[:, columns], updated_out.at[:, place], sems.at[SLABS + 3 + k]
+        )
+
+    def late_update(k, carry):
+        columns = pl.ds(pl.multiple_of(k * PB, PB), PB)
+        first = col_count - (KEEP - k) * PB
+        update_pair(
+            late,
+            columns,
+            updated,
+            pl.ds(pl.multiple_of(first, PB), PB),
+            parts,
+            late_raw[:, columns],
+            noise,
+            c * col_count + first - r * row_count,
+            r,
+        )
+        late_copy(k).start()
+        return carry
+
+    lax.fori_loop(0, KEEP, late_update, 0)
     height, width = error.shape
     target_covariance(
         error,
@@ -637,6 +728,8 @@
     )
     last = pltpu.make_async_copy(error, error_out, sems.at[SLABS + 2])
     last.start()
+    for k in range(KEEP):
+        copies.append(late_copy(k))
     for copy in copies:
         copy.wait()
     last.wait()
@@ -649,7 +742,7 @@
     row_count, col_count = covariance.shape
     target_width = targets.shape[1]
     error_rows = target_width * n_col // n_row
-    chunks = SPLIT * (target_width + col_count) // CHUNK
+    chunks = (target_width + col_count - PB) // CHUNK
 
     def f32(*shape):
         return jax.ShapeDtypeStruct(shape, jnp.float32)
@@ -665,9 +758,12 @@
             f32(row_count, target_width),
             f32(row_count, PB),
             f32(error_rows, target_width),
+            jax.ShapeDtypeStruct((row_count, 3 * PB), jnp.bfloat16),
+            f32(1, row_count),
+            f32(PB, KEEP * PB),
         ),
         in_specs=[anywhere] * 4,
-        out_specs=[vmem] * 4,
+        out_specs=[vmem] * 7,
         scratch_shapes=[
             pltpu.VMEM((row_count, PB), jnp.float32),
             pltpu.VMEM((PB, target_width + col_count), jnp.float32),
@@ -676,11 +772,9 @@
             pltpu.VMEM((PB,), jnp.int32),
             pltpu.VMEM((row_count,), jnp.int32),
             pltpu.SMEM(noise_var.shape, jnp.float32),
-            pltpu.VMEM((1, row_count), jnp.float32),
             pltpu.VMEM((HALF, PB), jnp.float32),
             pltpu.VMEM((PB, PB), jnp.float32),
             pltpu.VMEM((PB, PB), jnp.float32),
-            pltpu.VMEM((row_count, 3 * PB), jnp.bfloat16),
             pltpu.VMEM((3 * PB, 2 * PB), jnp.bfloat16),
             pltpu.VMEM((PB, target_width), jnp.float32),
             dma((11,)),
@@ -689,13 +783,15 @@
             dma((4,)),
             dma((chunks, 2)),
             dma((chunks,)),
+            dma((TAIL, 2)),
+            dma((TAIL,)),
             dma((ROW_CHUNKS, 2)),
             dma((ROW_CHUNKS, 2)),
             dma((n_col,)),
             dma,
         ],
         compiler_params=pltpu.CompilerParams(
-            collective_id=0, has_side_effects=True, vmem_limit_bytes=16 * 1024 * 1024
+            collective_id=0, has_side_effects=True, vmem_limit_bytes=14 * 1024 * 1024
         ),
         name="panel",
     )(
@@ -711,10 +807,14 @@
             f32(row_count, PB),
             f32(error_rows, target_width),
         ),
-        in_specs=[vmem] * 5 + [smem] * 3,
+        in_specs=[vmem] * 8 + [smem] * 3,
         out_specs=[anywhere] * 4,
-        scratch_shapes=[pltpu.VMEM((error_rows, target_width), jnp.float32), dma((SLABS + 3,))],
-        compiler_params=pltpu.CompilerParams(vmem_limit_bytes=4 * 1024 * 1024),
+        scratch_shapes=[
+            pltpu.VMEM((error_rows, target_width), jnp.float32),
+            pltpu.VMEM((row_count, KEEP * PB), jnp.float32),
+            dma((SLABS + 3 + KEEP,)),
+        ],
+        compiler_params=pltpu.CompilerParams(vmem_limit_bytes=8 * 1024 * 1024),
         name="store",
     )(*results, target_pos, layer_strength, layer_scale, tile_layer)
     updated, reconstructor, panel, error_cov = outs

time: 69.1 us -> 67.8 us (0.981)
  Pallas kernels: 68.2 us -> 66.9 us
    pallas_call x1, Pallas kernels: 59.5 us -> 58.2 us  [local(): pl.pallas_call(functools.partial(panel_kernel, n_row, n_col), out_shape=(...]
where the time goes in v4:
time: 67.8 us; the launch traced here: 67.6 us
  Pallas kernels  66.9 us (99%)
  between operations  0.7 us (1%)
    pallas_call x1, Pallas kernels, local(): pl.pallas_call(functools.partial(panel_kernel, n_row, n_col), out_shape=(...  58.2 us
    pallas_call x1, Pallas kernels, local(): pl.pallas_call(store_kernel, out_shape=(f32(row_count, col_count), f32(ro...  8.68 us

profile of v4, /device:TPU:31, one launch (start us, length us, event | category | flops | bytes accessed | tf_op | source)
XLA Modules:
  0.0 67.6 jit_solution(10490515531843051242)
XLA Ops:
  0.6 0.0 copy-start.3
  0.6 0.0 copy-start.2
  0.7 0.0 copy-start.1
  0.7 0.0 copy-start
  0.7 58.2 %panel.1 = (f32[1536,3072]{1,0:T(8,128)S(1)}, f32[1536,512]{1,0:T(8,128)S(1)}, f32[1536,256]{1,0:T(8,128)S(1)}, f32[256,512]{1,0:T(8,128)S(1)}, bf16[1536,768]{1...) custom-call(f32[1536,3072]{1,0:T(8,128)} %cov.1, f32[1536,512]{1,0:T(8,128)} %targets.1, ...), custom_call_target="tpu_custom_call" | custom-call | tf_op jit(solution)/shard_map/panel/pallas_call | solution.py:754
  58.9 0.0 copy-done.3
  58.9 0.0 copy-done.2
  58.9 0.0 copy-done.1
  58.9 0.0 copy-done
  58.9 8.7 %store.1 = (f32[1536,3072]{1,0:T(8,128)}, f32[1536,512]{1,0:T(8,128)}, f32[1536,256]{1,0:T(8,128)}, f32[256,512]{1,0:T(8,128)}) custom-call(f32[1536,3072]{1,0:T(8,128)S(1)} %get-tuple-element.15.updated, f32[1536,512]{1,0:T(8,128)S(1)} %get-tuple-element.16.reconstructor, f32[1536,256]{1,0:T(8,128)S(1)} %get-tuple-element.17.panel, ...), custom_call_target="tpu_custom_call" | custom-call | tf_op jit(solution)/shard_map/store/pallas_call | solution.py:802
Async XLA Ops:
  0.6 58.3 %copy-start.3 = (s32[16]{0:T(128)S(1)}, s32[16]{0:T(128)}, u32[]{:S(2)}) copy-start(s32[16]{0:T(128)} %tile_layer.1) | copy-start | bytes 196
  0.6 58.3 %copy-start.2 = (f32[35]{0:T(128)S(1)}, f32[35]{0:T(128)}, u32[]{:S(2)}) copy-start(f32[35]{0:T(128)} %scale.1) | copy-start | bytes 424
  0.7 58.3 %copy-start.1 = (f32[35]{0:T(128)S(1)}, f32[35]{0:T(128)}, u32[]{:S(2)}) copy-start(f32[35]{0:T(128)} %strength.1) | copy-start | bytes 424
  0.7 58.3 %copy-start = (f32[2,2048]{1,0:T(2,128)S(1)}, f32[2,2048]{1,0:T(2,128)}, u32[]{:S(2)}) copy-start(f32[2,2048]{1,0:T(2,128)} %pos.1) | copy-start | bytes 49156
